TPU v7x, 512 devices: a whole 4x8x8 slice. The times are simulated.
512 devices in a mesh: vocab: 64 (over y, x, core), width: 8 (over z).
Axes of the slice: x: 4, y: 8, z: 8, core: 2. Of those that a mesh axis runs over, the one named last changes fastest.
Arguments:
- hidden: bfloat16 [8192, 2048], P('vocab', 'width'), may hold values from -400 to 400
- norm_gain: bfloat16 [2048], P('width'), may hold values from 0.5 to 1.5
- head_weight: bfloat16 [102400, 2048], P('vocab', 'width'), may hold values from -1 to 1
- targets: int32 [8192], P(('vocab', 'width')), may hold values from 0 to 102399
- pad_mask: int32 [8192], P(('vocab', 'width')), may hold values 0 or 1
- lengths: int32 [64], replicated, may hold values from 1 to 2048, 8192 in all
Outputs:
- entropy: float32 [8192], P(('vocab', 'width'))
- token_logprob: float32 [8192], P(('vocab', 'width'))
- seq_score: float32 [64], replicated
Inputs may be any that keep to these rules, and one draw needn't show every extreme that they name: The lengths sum to 8192.
All inputs are finite; a program needn't handle non-finite values. No bound on the sum of `pad_mask` on one device may be relied on, other than what follows from the above.
Results may differ from a plain program's by a relative error of at most 0.0031.
Values may be sent and summed in bfloat16 or wider, within the bound.
A program may use at most 64 MiB of HBM per device.

v0:
```python
import math
import jax
import jax.numpy as jnp
from jax import lax
from jax.sharding import PartitionSpec as P

epsilon = 1e-06


def merged_2(value, axis, join):
    pieces = jax.tree.map(lambda part: lax.all_gather(part, axis), value)
    head = jax.tree.map(lambda part: part[0], pieces)
    tail = jax.tree.map(lambda part: part[1:], pieces)
    total, _ = lax.scan(lambda total, piece: (join(total, piece), None), head, tail)
    return total


def summarize(logits, block_ids, first_col):
    peak = jnp.max(logits, axis=1)
    shifted = logits - peak[:, None]
    weights = jnp.exp(shifted)
    exp_total = jnp.sum(weights, axis=1)
    spread = jnp.sum(weights * shifted, axis=1)
    columns = first_col + lax.iota(jnp.int32, logits.shape[1])
    target_logit = jnp.sum(jnp.where(columns[None, :] == block_ids[:, None], logits, 0.0), axis=1)
    return (peak, exp_total, spread, target_logit)


def combine(earlier, later):
    peak = jnp.maximum(earlier[0], later[0])
    left_lift = jnp.exp(earlier[0] - peak)
    right_lift = jnp.exp(later[0] - peak)
    exp_total = earlier[1] * left_lift + later[1] * right_lift
    spread = left_lift * (earlier[2] + (earlier[0] - peak) * earlier[1]) + right_lift * (
        later[2] + (later[0] - peak) * later[1]
    )
    return (peak, exp_total, spread, earlier[3] + later[3])


def per_device(hidden, norm_gain, head_weight, targets, pad_mask, lengths):
    width_count = lax.axis_size("width")
    own_count = targets.shape[0]
    values = hidden.astype(jnp.float32)
    energy = lax.psum(jnp.sum(values * values, axis=1), "width")
    inv_rms = lax.rsqrt(energy / (hidden.shape[1] * width_count) + epsilon)
    normed = (values * inv_rms[:, None] * norm_gain.astype(jnp.float32)[None, :]).astype(
        jnp.bfloat16
    )
    full_rows = lax.all_to_all(normed, "width", split_axis=0, concat_axis=1, tiled=True)
    gathered, gathered_ids = (
        lax.all_gather(full_rows, "vocab", axis=0, tiled=True),
        lax.all_gather(targets, "vocab", axis=0, tiled=True),
    )
    col_count = head_weight.shape[0]
    first_col = lax.axis_index("vocab") * col_count
    total_rows = gathered.shape[0]
    block_rows = math.gcd(total_rows, 512)
    contract = (((1,), (1,)), ((), ()))
    head_full = lax.all_gather(head_weight, "width", axis=1, tiled=True)

    def per_block(inputs):
        logits = lax.dot_general(inputs[0], head_full, contract, preferred_element_type=jnp.float32)
        return summarize(logits, inputs[1], first_col)

    blocked = lax.map(
        per_block,
        (gathered.reshape(-1, block_rows, gathered.shape[1]), gathered_ids.reshape(-1, block_rows)),
    )
    statistics = (
        blocked[0].reshape(-1),
        blocked[1].reshape(-1),
        blocked[2].reshape(-1),
        blocked[3].reshape(-1),
    )
    merged = merged_2(statistics, "vocab", combine)
    own_start = lax.axis_index("vocab") * own_count
    peak = lax.dynamic_slice_in_dim(merged[0], own_start, own_count, 0)
    exp_total = lax.dynamic_slice_in_dim(merged[1], own_start, own_count, 0)
    spread = lax.dynamic_slice_in_dim(merged[2], own_start, own_count, 0)
    target_logit = lax.dynamic_slice_in_dim(merged[3], own_start, own_count, 0)
    kept_mask = pad_mask.astype(jnp.float32)
    log_total = jnp.log(exp_total)
    entropy = kept_mask * (log_total - spread / exp_total)
    token_logprob = kept_mask * (target_logit - peak - log_total)
    device_index = lax.axis_index("vocab") * width_count + lax.axis_index("width")
    token_index = device_index * own_count + lax.iota(jnp.int32, own_count)
    seq_ends = jnp.cumsum(lengths)
    seq_starts = seq_ends - lengths
    member = (
        (token_index[:, None] >= seq_starts[None, :]) & (token_index[:, None] < seq_ends[None, :])
    ).astype(jnp.float32)
    partial_value = jnp.sum(member * token_logprob[:, None], axis=0)
    seq_score = lax.psum(partial_value, ("vocab", "width")) / lengths.astype(jnp.float32)
    return (entropy, token_logprob, seq_score)


def solution(mesh):
    placed = (
        P("vocab", "width"),
        P("width"),
        P("vocab", "width"),
        P(("vocab", "width")),
        P(("vocab", "width")),
        P(),
    )
    return jax.shard_map(
        per_device,
        mesh=mesh,
        in_specs=placed,
        out_specs=(P(("vocab", "width")), P(("vocab", "width")), P()),
        check_vma=False,
    )
```

profile of v0, /device:TPU:1, one launch (start us, length us, event | category | flops | bytes accessed | tf_op | source)
XLA Modules:
  0.0 491.1 jit_solution(4575408305845917003)
XLA Ops:
  7.2 0.0 all-gather.7.cloned.1.call-start
  7.2 0.9 fusion.5
  8.2 20.3 %psum.14 = f32[128]{0:T(128)S(1)} all-reduce(f32[128]{0:T(128)S(1)} %fusion.5), channel_id=1, replica_groups=mesh['vocab'=64,'width'=8] {'width'}, use_global_device_ids=true, to_apply=%region_1.0 | all-reduce | flops 128 | bytes 1024 | tf_op jit(solution)/shard_map/psum | solution.py:44
  28.4 0.7 convert_element_type.18
  29.1 0.9 fusion.7
  30.0 9.6 %all_to_all.19 = bf16[8,16,256]{2,1,0:T(8,128)(2,1)S(1)} all-to-all(bf16[8,16,256]{2,1,0:T(8,128)(2,1)S(1)} %bitcast.73), channel_id=1, replica_groups=mesh['vocab'=64,'width'=8] {'width'}, dimensions={0} | all-to-all | bytes 131072 | tf_op jit(solution)/shard_map/all_to_all | solution.py:49
  39.6 0.6 copy.21
  40.2 0.0 all-gather.7.cloned.1.call-update
  40.3 0.0 all-gather.9.cloned.1.call-start
  40.3 0.7 all-gather.9.cloned.1.call-update
  41.1 1.3 dynamic-slice
  43.0 0.9 dynamic-update-slice
  43.9 22.5 %all-reduce = s32[1024]{0:T(1024)S(1)} all-reduce(s32[1024]{0:T(1024)S(1)} %dynamic-update-slice), channel_id=1, replica_groups=mesh['vocab'=64,'width'=8] {'vocab'}, use_global_device_ids=true, to_apply=%add | all-reduce | flops 1024 | bytes 8192
  66.4 0.7 copy.16
  67.2 0.1 reduce-window.8
  67.3 0.1 reduce
  67.4 0.7 sub.31
  68.0 58.4 %all-gather.7.cloned.1.call-done = bf16[1024,2048]{1,0:T(8,128)(2,1)} async-done(((bf16[16,2048]{1,0:T(8,128)(2,1)}), bf16[1024,2048]{1,0:T(8,128)(2,1)}) %all-gather.7.cloned.1.call-update) | async-done | bytes 4194320 | tf_op jit(solution)/shard_map/all_gather | solution.py:51
  126.4 83.2 %all-gather.9.cloned.1.call-done = bf16[1600,2048]{1,0:T(8,128)(2,1)} async-done(((bf16[1600,256]{1,0:T(8,128)(2,1)}), bf16[1600,2048]{1,0:T(8,128)(2,1)}) %all-gather.9.cloned.1.call-update) | async-done | bytes 6553616 | tf_op jit(solution)/shard_map/all_gather | solution.py:59
  209.6 16.2 %while.32 = (s32[]{:T(128)}, f32[2,512]{1,0:T(2,128)S(1)}, f32[2,512]{1,0:T(2,128)S(1)}, f32[2,512]{1,0:T(2,128)S(1)}, f32[2,512]{1,0:T(2,128)S(1)}, /*index=5*/...) while((s32[]{:T(128)}, f32[2,512]{1,0:T(2,128)S(1)}, ...), condition=%wide.region_7.8_spmd, body=%wide.region_2.7_spmd.sunk | while | flops 3361996288 | bytes 15250565 | solution.py:65
  209.6 6.4 %fusion.14 = (f32[512]{0:T(512)S(1)}, f32[512,1600]{0,1:T(8,128)S(1)}) fusion(bf16[1600,2048]{1,0:T(8,128)(2,1)} %get-tuple-element.320, bf16[2,512,2048]{2,1,0:T(8,128)(2,1)} %get-tuple-element.319, s32[]{:T(128)} %get-tuple-element.303), kind=kOutput, calls=%fused_computation.31.clone.1 | convolution fusion | flops 3356261888 | bytes 11930112 | tf_op jit(solution)/shard_map/while/body/eval_jaxpr/dot_general | solution.py:62
  216.1 1.4 fusion.15
  217.7 6.4 %fusion.14 = (f32[512]{0:T(512)S(1)}, f32[512,1600]{0,1:T(8,128)S(1)}) fusion(bf16[1600,2048]{1,0:T(8,128)(2,1)} %get-tuple-element.320, bf16[2,512,2048]{2,1,0:T(8,128)(2,1)} %get-tuple-element.319, s32[]{:T(128)} %get-tuple-element.303), kind=kOutput, calls=%fused_computation.31.clone.1 | convolution fusion | flops 3356261888 | bytes 11930112 | tf_op jit(solution)/shard_map/while/body/eval_jaxpr/dot_general | solution.py:62
  224.2 1.4 fusion.15
  225.8 0.0 copy-start.2
  225.8 0.0 copy-start.1
  225.8 42.7 %all-gather = f32[64,1,1024]{2,1,0:T(1,128)S(1)} all-gather(f32[1,1,1024]{2,1,0:T(1,128)S(1)} %reshape.60), channel_id=1, replica_groups=mesh['vocab'=64,'width'=8] {'vocab'}, dimensions={0}, use_global_device_ids=true | all-gather | bytes 266240 | tf_op jit(solution)/shard_map/all_gather | solution.py:11
  268.6 37.2 %all-gather.1 = f32[64,1,1024]{2,1,0:T(1,128)S(1)} all-gather(f32[1,1,1024]{2,1,0:T(1,128)S(1)} %reshape.62), channel_id=1, replica_groups=mesh['vocab'=64,'width'=8] {'vocab'}, dimensions={0}, use_global_device_ids=true | all-gather | bytes 266240 | tf_op jit(solution)/shard_map/all_gather | solution.py:11
  305.8 36.9 %all-gather.2 = f32[64,1,1024]{2,1,0:T(1,128)S(1)} all-gather(f32[1,1,1024]{2,1,0:T(1,128)S(1)} %reshape.64), channel_id=1, replica_groups=mesh['vocab'=64,'width'=8] {'vocab'}, dimensions={0}, use_global_device_ids=true | all-gather | bytes 266240 | tf_op jit(solution)/shard_map/all_gather | solution.py:11
  342.7 37.1 %all-gather.3 = f32[64,1,1024]{2,1,0:T(1,128)S(1)} all-gather(f32[1,1,1024]{2,1,0:T(1,128)S(1)} %reshape.66), channel_id=1, replica_groups=mesh['vocab'=64,'width'=8] {'vocab'}, dimensions={0}, use_global_device_ids=true | all-gather | bytes 266240 | tf_op jit(solution)/shard_map/all_gather | solution.py:11
  380.2 7.6 %while.33 = (s32[]{:T(128)}, f32[1024]{0:T(1024)S(1)}, f32[1024]{0:T(1024)S(1)}, f32[1024]{0:T(1024)S(1)}, f32[1024]{0:T(1024)S(1)}, /*index=5*/f32[63,1024]{1,0...) while((s32[]{:T(128)}, f32[1024]{0:T(1024)S(1)}, ...), condition=%wide.region_9.10_spmd, body=%wide.region_8.9_spmd.sunk | while | flops 16386 | bytes 110701 | solution.py:14
  387.7 0.0 copy-done.2
  387.7 0.6 subtract_multiply_fusion
  388.3 0.0 copy-start
  388.3 0.1 select_reduce_fusion.1
  388.4 95.3 %psum.15 = f32[64]{0:T(128)S(1)} all-reduce(f32[64]{0:T(128)S(1)} %select_reduce_fusion.1), channel_id=1, replica_groups=mesh['vocab'=64,'width'=8] {'vocab','width'}, use_global_device_ids=true, to_apply=%region_12.13 | all-reduce | flops 64 | bytes 512 | tf_op jit(solution)/shard_map/psum | solution.py:93
  483.7 0.0 copy-done.1
  483.7 0.5 convert_divide_fusion
  484.2 0.0 copy-done
  (414 shorter events, 4.6 us)
Async XLA Ops:
  7.2 119.3 %all-gather.7.cloned.1.call-start = ((), (), s32[]{:S(2)}) async-start(), calls=%async_computation.1 | async-start | bytes 4259840 | tf_op jit(solution)/shard_map/all_gather | solution.py:51
  40.3 169.3 %all-gather.9.cloned.1.call-start = ((), (), s32[]{:S(2)}) async-start(), calls=%async_computation.2 | async-start | bytes 7372800 | tf_op jit(solution)/shard_map/all_gather | solution.py:59
  225.8 162.0 %copy-start.2 = (s32[16]{0:T(128)S(1)}, s32[16]{0:T(128)}, u32[]{:S(2)}) copy-start(s32[16]{0:T(128)} %param.14) | copy-start | bytes 196
  225.8 257.9 %copy-start.1 = (s32[64]{0:T(128)S(1)}, s32[64]{0:T(128)}, u32[]{:S(2)}) copy-start(s32[64]{0:T(128)} %param.15) | copy-start | bytes 772
  388.3 95.9 %copy-start = (f32[16]{0:T(128)}, f32[16]{0:T(128)S(1)}, u32[]{:S(2)}) copy-start(f32[16]{0:T(128)S(1)} %get-tuple-element.158) | copy-start | bytes 196
Sparse Core Ops, SparseCore 0:
  40.4 85.9 all-gather.6
  128.4 81.1 all-gather.8
where the time goes:
time: 491 us
  blocking collectives  302 us (62%)
  waiting for transfers between devices  142 us (29%)
  between operations  14.9 us (3%)
  matrix products  12.9 us (3%)
  other arithmetic  9.19 us (2%)
  local copies, waits for them, and re-layouts  6.36 us (1%)
    all_gather x4, blocking collectives, merged_2(): pieces = jax.tree.map(lambda part: lax.all_gather(part, axis), value)  154 us
    psum x1, blocking collectives, per_device(): lax.psum(partial_value, ('vocab', 'width')) / lengths.astype(jnp.float32)  95.3 us
    all_gather x1, waiting for transfers between devices, per_device(): head_full = lax.all_gather(head_weight, 'width', axis=1, tiled=True)  83.2 us
    all_gather x1, waiting for transfers between devices, per_device(): lax.all_gather(full_rows, 'vocab', axis=0, tiled=True)  58.4 us
    unnamed x1, blocking collectives  22.5 us
    psum x1, blocking collectives, per_device(): energy = lax.psum(jnp.sum(values * values, axis=1), 'width')  20.3 us
    dot_general x2, matrix products, per_block(): lax.dot_general(inputs[0], head_full, contract, preferred_element_type=jn...  12.9 us
  transfers between devices with their start and end apart: 2, of which 2 were waited for; matrix products, arithmetic and copies ran while one was open for 1% of the time, Pallas kernels for 0%

commit v1 on v0

--- a/solution.py
+++ b/solution.py
@@ -5,6 +5,12 @@
 from jax.sharding import PartitionSpec as P
 
 epsilon = 1e-06
+
+
+def in_order(blocks, dim):
+    shape = list(blocks.shape[1:])
+    shape[dim] *= blocks.shape[0]
+    return jnp.moveaxis(blocks, 0, dim).reshape(shape)
 
 
 def merged_2(value, axis, join):
@@ -56,7 +62,19 @@
     total_rows = gathered.shape[0]
     block_rows = math.gcd(total_rows, 512)
     contract = (((1,), (1,)), ((), ()))
-    head_full = lax.all_gather(head_weight, "width", axis=1, tiled=True)
+    devices = lax.axis_size("width")
+    pairs = [(i, (i + 1) % devices) for i in range(devices)]
+    back = [(b, a) for a, b in pairs]
+    lower, upper = ([], [])
+    for step in range(devices - 1):
+        if step % 2 == 0:
+            lower.append(lax.ppermute(lower[-1] if lower else head_weight, "width", pairs))
+        else:
+            upper.append(lax.ppermute(upper[-1] if upper else head_weight, "width", back))
+    blocks = jnp.stack([*lower[::-1], head_weight, *upper])
+    shift = lax.axis_index("width") - len(lower)
+    blocks = blocks[(jnp.arange(devices) - shift) % devices]
+    head_full = in_order(blocks, 1)
 
     def per_block(inputs):
         logits = lax.dot_general(inputs[0], head_full, contract, preferred_element_type=jnp.float32)

time: 491 us -> 442 us (0.900)
  waiting for transfers between devices: 142 us -> 39.7 us
  local copies, waits for them, and re-layouts: 6.36 us -> 30.4 us
  starting transfers between devices: 0.08 us -> 22.2 us
  blocking collectives: 302 us -> 307 us
    all_gather x1 -> x0, waiting for transfers between devices: 83.2 us -> none  [per_device(): head_full = lax.all_gather(head_weight, 'width', axis=1, tiled=True)]
    all_gather x1, waiting for transfers between devices: 58.4 us -> 0.01 us  [per_device(): lax.all_gather(full_rows, 'vocab', axis=0, tiled=True)]
    ppermute x0 -> x7, waiting for transfers between devices: none -> 39.7 us  [the longest x4 35.5 us: per_device(): lax.ppermute(lower[-1] if lower else head_weight, 'width', pairs)]
    ppermute x0 -> x7, starting transfers between devices: none -> 22.2 us  [the longest x3 14.3 us: per_device(): lax.ppermute(upper[-1] if upper else head_weight, 'width', back)]
    unnamed x17 -> x26, local copies, waits for them, and re-layouts: 2.41 us -> 12.5 us
    gather x0 -> x1, local copies, waits for them, and re-layouts: none -> 6.52 us  [per_device(): blocks = blocks[(jnp.arange(devices) - shift) % devices]]
    reshape x0 -> x1, local copies, waits for them, and re-layouts: none -> 6.52 us  [in_order(): return jnp.moveaxis(blocks, 0, dim).reshape(shape)]
    unnamed x1, blocking collectives: 22.5 us -> 27.8 us
  transfers between devices with their start and end apart: 2 -> 8, of which waited for: 2 -> 4; matrix products, arithmetic and copies ran while one was open for 1% -> 6% of each run, Pallas kernels for 0% -> 0%
where the time goes in v1:
time: 442 us; the launch traced here: 441 us
  blocking collectives  307 us (69%)
  waiting for transfers between devices  39.7 us (9%)
  local copies, waits for them, and re-layouts  30.4 us (7%)
  starting transfers between devices  22.2 us (5%)
  between operations  15 us (3%)
  matrix products  12.9 us (3%)
  other arithmetic  9.28 us (2%)
    all_gather x4, blocking collectives, merged_2(): pieces = jax.tree.map(lambda part: lax.all_gather(part, axis), value)  153 us
    psum x1, blocking collectives, per_device(): lax.psum(partial_value, ('vocab', 'width')) / lengths.astype(jnp.float32)  96.9 us
    ppermute x4, waiting for transfers between devices, per_device(): lax.ppermute(lower[-1] if lower else head_weight, 'width', pairs)  35.5 us
    unnamed x1, blocking collectives  27.8 us
    psum x1, blocking collectives, per_device(): energy = lax.psum(jnp.sum(values * values, axis=1), 'width')  20.3 us
    ppermute x3, starting transfers between devices, per_device(): lax.ppermute(upper[-1] if upper else head_weight, 'width', back)  14.3 us
    dot_general x2, matrix products, per_block(): lax.dot_general(inputs[0], head_full, contract, preferred_element_type=jn...  12.9 us
    unnamed x26, local copies, waits for them, and re-layouts  12.5 us
  transfers between devices with their start and end apart: 8, of which 4 were waited for; matrix products, arithmetic and copies ran while one was open for 6% of the time, Pallas kernels for 0%

profile of v1, /device:TPU:1, one launch (start us, length us, event | category | flops | bytes accessed | tf_op | source)
XLA Modules:
  0.0 440.7 jit_solution(9112587625399733994)
XLA Ops:
  7.2 0.0 copy-start
  7.2 0.0 all-gather.6.cloned.1.call-start
  7.2 1.0 fusion.5
  8.2 20.3 %psum.14 = f32[128]{0:T(128)S(1)} all-reduce(f32[128]{0:T(128)S(1)} %fusion.5), channel_id=1, replica_groups=mesh['vocab'=64,'width'=8] {'width'}, use_global_device_ids=true, to_apply=%region_1.0 | all-reduce | flops 128 | bytes 1024 | tf_op jit(solution)/shard_map/psum | solution.py:50
  28.5 0.7 convert_element_type.18
  29.2 0.9 fusion.7
  30.1 9.6 %all_to_all.19 = bf16[8,16,256]{2,1,0:T(8,128)(2,1)S(1)} all-to-all(bf16[8,16,256]{2,1,0:T(8,128)(2,1)S(1)} %bitcast.96), channel_id=1, replica_groups=mesh['vocab'=64,'width'=8] {'width'}, dimensions={0} | all-to-all | bytes 131072 | tf_op jit(solution)/shard_map/all_to_all | solution.py:55
  39.7 0.6 copy.25
  40.3 0.0 all-gather.6.cloned.1.call-update
  40.3 2.2 collective-permute-start
  42.6 15.0 %collective-permute-done = bf16[1600,256]{1,0:T(8,128)(2,1)S(1)} collective-permute-done((bf16[1600,256]{1,0:T(8,128)(2,1)}, bf16[1600,256]{1,0:T(8,128)(2,1)S(1)}, u32[]{:S(2)}, u32[]{:S(2)}) %collective-permute-start) | collective-permute-done | bytes 819232 | tf_op jit(solution)/shard_map/ppermute | solution.py:71
  57.6 1.9 collective-permute-start.1
  59.5 4.6 %collective-permute-start.4 = (bf16[1600,256]{1,0:T(8,128)(2,1)}, bf16[1600,256]{1,0:T(8,128)(2,1)S(1)}, u32[]{:S(2)}, u32[]{:S(2)}) collective-permute-start(bf16[1600,256]{1,0:T(8,128)(2,1)} %param.12), channel_id=1, source_target_pairs={{1,0},{2,1},{3,2},{4,3},{5,4},{6,5},{7,6},{0,7},{9,8},{10,9},{11,1... | collective-permute-start | bytes 2457608 | tf_op jit(solution)/shard_map/ppermute | solution.py:73
  64.1 10.2 %collective-permute-done.1 = bf16[1600,256]{1,0:T(8,128)(2,1)S(1)} collective-permute-done((bf16[1600,256]{1,0:T(8,128)(2,1)S(1)}, bf16[1600,256]{1,0:T(8,128)(2,1)S(1)}, u32[]{:S(2)}, u32[]{:S(2)}) %collective-permute-start.1) | collective-permute-done | bytes 819232 | tf_op jit(solution)/shard_map/ppermute | solution.py:71
  74.3 1.9 collective-permute-start.2
  76.2 0.0 collective-permute-done.4
  76.2 4.6 %collective-permute-start.5 = (bf16[1600,256]{1,0:T(8,128)(2,1)S(1)}, bf16[1600,256]{1,0:T(8,128)(2,1)}, u32[]{:S(2)}, u32[]{:S(2)}) collective-permute-start(bf16[1600,256]{1,0:T(8,128)(2,1)S(1)} %collective-permute-done.4), channel_id=1, source_target_pairs={{1,0},{2,1},{3,2},{4,3},{5,4},{6,5},{7,6},{0,7},{9,8},{10,9},{11,1... | collective-permute-start | bytes 2457608 | tf_op jit(solution)/shard_map/ppermute | solution.py:73
  80.8 10.3 %collective-permute-done.2 = bf16[1600,256]{1,0:T(8,128)(2,1)} collective-permute-done((bf16[1600,256]{1,0:T(8,128)(2,1)S(1)}, bf16[1600,256]{1,0:T(8,128)(2,1)}, u32[]{:S(2)}, u32[]{:S(2)}) %collective-permute-start.2) | collective-permute-done | bytes 819232 | tf_op jit(solution)/shard_map/ppermute | solution.py:71
  91.1 1.9 collective-permute-start.3
  93.0 1.3 dynamic-slice
  95.0 0.9 dynamic-update-slice
  95.8 27.8 %all-reduce = s32[1024]{0:T(1024)S(1)} all-reduce(s32[1024]{0:T(1024)S(1)} %dynamic-update-slice), channel_id=1, replica_groups=mesh['vocab'=64,'width'=8] {'vocab'}, use_global_device_ids=true, to_apply=%add | all-reduce | flops 1024 | bytes 8192
  123.7 0.7 copy.20
  124.4 0.1 reduce-window.8
  124.5 0.1 reduce
  124.6 0.7 sub.50
  125.4 0.0 collective-permute-done.5
  125.4 5.1 %collective-permute-start.6 = (bf16[1600,256]{1,0:T(8,128)(2,1)}, bf16[1600,256]{1,0:T(8,128)(2,1)S(1)}, u32[]{:S(2)}, u32[]{:S(2)}) collective-permute-start(bf16[1600,256]{1,0:T(8,128)(2,1)} %collective-permute-done.5), channel_id=1, source_target_pairs={{1,0},{2,1},{3,2},{4,3},{5,4},{6,5},{7,6},{0,7},{9,8},{10,9},{11,1... | collective-permute-start | bytes 2457608 | tf_op jit(solution)/shard_map/ppermute | solution.py:73
  130.5 0.0 collective-permute-done.3
  130.5 2.1 bitcast_dynamic-update-slice_fusion.7
  132.6 2.1 bitcast_dynamic-update-slice_fusion.6
  134.7 1.0 bitcast_dynamic-update-slice_fusion.5
  135.7 0.9 bitcast_dynamic-update-slice_fusion.4
  136.6 0.0 copy-done
  136.6 0.9 bitcast_dynamic-update-slice_fusion.3
  137.6 0.9 bitcast_dynamic-update-slice_fusion.2
  138.5 2.1 bitcast_dynamic-update-slice_fusion.1
  140.6 4.1 collective-permute-done.6
  144.8 0.9 bitcast_dynamic-update-slice_fusion
  145.7 6.5 %gather_fusion = bf16[8,1600,256]{2,1,0:T(8,128)(2,1)} fusion(bf16[8,1600,256]{2,1,0:T(8,128)(2,1)} %bitcast_dynamic-update-slice_fusion, s32[1024]{0:T(1024)S(1)} %pad_clamp_fusion), kind=kCustom, calls=%fused_computation | custom fusion | bytes 13107232 | tf_op jit(solution)/shard_map/gather | solution.py:76
  152.2 6.5 %copy.26 = bf16[8,200,8,256]{3,2,0,1:T(8,128)(2,1)} copy(bf16[8,200,8,256]{3,2,1,0:T(8,128)(2,1)} %bitcast.81) | data formatting | bytes 13107200 | tf_op jit(solution)/shard_map/reshape | solution.py:13
  158.8 0.0 all-gather.6.cloned.1.call-done
  158.8 0.0 copy-start.3
  158.8 0.0 copy-start.2
  158.8 16.2 %while.32 = (s32[]{:T(128)}, f32[2,512]{1,0:T(2,128)S(1)}, f32[2,512]{1,0:T(2,128)S(1)}, f32[2,512]{1,0:T(2,128)S(1)}, f32[2,512]{1,0:T(2,128)S(1)}, /*index=5*/...) while((s32[]{:T(128)}, f32[2,512]{1,0:T(2,128)S(1)}, ...), condition=%wide.region_7.8_spmd, body=%wide.region_2.7_spmd.sunk | while | flops 3361996288 | bytes 15250565 | solution.py:83
  158.8 6.5 %fusion.16 = (f32[512]{0:T(512)S(1)}, f32[512,1600]{0,1:T(8,128)S(1)}) fusion(bf16[1600,2048]{1,0:T(8,128)(2,1)} %get-tuple-element.320, bf16[2,512,2048]{2,1,0:T(8,128)(2,1)} %get-tuple-element.319, s32[]{:T(128)} %get-tuple-element.303), kind=kOutput, calls=%fused_computation.47.clone.1 | convolution fusion | flops 3356261888 | bytes 11930112 | tf_op jit(solution)/shard_map/while/body/eval_jaxpr/dot_general | solution.py:80
  165.3 1.4 fusion.17
  166.9 6.4 %fusion.16 = (f32[512]{0:T(512)S(1)}, f32[512,1600]{0,1:T(8,128)S(1)}) fusion(bf16[1600,2048]{1,0:T(8,128)(2,1)} %get-tuple-element.320, bf16[2,512,2048]{2,1,0:T(8,128)(2,1)} %get-tuple-element.319, s32[]{:T(128)} %get-tuple-element.303), kind=kOutput, calls=%fused_computation.47.clone.1 | convolution fusion | flops 3356261888 | bytes 11930112 | tf_op jit(solution)/shard_map/while/body/eval_jaxpr/dot_general | solution.py:80
  173.3 1.4 fusion.17
  174.9 41.4 %all-gather = f32[64,1,1024]{2,1,0:T(1,128)S(1)} all-gather(f32[1,1,1024]{2,1,0:T(1,128)S(1)} %reshape.121), channel_id=1, replica_groups=mesh['vocab'=64,'width'=8] {'vocab'}, dimensions={0}, use_global_device_ids=true | all-gather | bytes 266240 | tf_op jit(solution)/shard_map/all_gather | solution.py:17
  216.4 37.1 %all-gather.1 = f32[64,1,1024]{2,1,0:T(1,128)S(1)} all-gather(f32[1,1,1024]{2,1,0:T(1,128)S(1)} %reshape.123), channel_id=1, replica_groups=mesh['vocab'=64,'width'=8] {'vocab'}, dimensions={0}, use_global_device_ids=true | all-gather | bytes 266240 | tf_op jit(solution)/shard_map/all_gather | solution.py:17
  253.6 36.9 %all-gather.2 = f32[64,1,1024]{2,1,0:T(1,128)S(1)} all-gather(f32[1,1,1024]{2,1,0:T(1,128)S(1)} %reshape.125), channel_id=1, replica_groups=mesh['vocab'=64,'width'=8] {'vocab'}, dimensions={0}, use_global_device_ids=true | all-gather | bytes 266240 | tf_op jit(solution)/shard_map/all_gather | solution.py:17
  290.6 37.3 %all-gather.3 = f32[64,1,1024]{2,1,0:T(1,128)S(1)} all-gather(f32[1,1,1024]{2,1,0:T(1,128)S(1)} %reshape.127), channel_id=1, replica_groups=mesh['vocab'=64,'width'=8] {'vocab'}, dimensions={0}, use_global_device_ids=true | all-gather | bytes 266240 | tf_op jit(solution)/shard_map/all_gather | solution.py:17
  328.2 7.6 %while.33 = (s32[]{:T(128)}, f32[1024]{0:T(1024)S(1)}, f32[1024]{0:T(1024)S(1)}, f32[1024]{0:T(1024)S(1)}, f32[1024]{0:T(1024)S(1)}, /*index=5*/f32[63,1024]{1,0...) while((s32[]{:T(128)}, f32[1024]{0:T(1024)S(1)}, ...), condition=%wide.region_9.10_spmd, body=%wide.region_8.9_spmd.sunk | while | flops 16386 | bytes 110701 | solution.py:20
  335.7 0.0 copy-done.3
  335.7 0.6 subtract_multiply_fusion
  336.3 0.0 copy-start.1
  336.3 0.1 select_reduce_fusion.1
  336.4 96.9 %psum.15 = f32[64]{0:T(128)S(1)} all-reduce(f32[64]{0:T(128)S(1)} %select_reduce_fusion.1), channel_id=1, replica_groups=mesh['vocab'=64,'width'=8] {'vocab','width'}, use_global_device_ids=true, to_apply=%region_12.13 | all-reduce | flops 64 | bytes 512 | tf_op jit(solution)/shard_map/psum | solution.py:111
  433.3 0.0 copy-done.2
  433.3 0.5 convert_divide_fusion
  433.9 0.0 copy-done.1
  (416 shorter events, 4.6 us)
Async XLA Ops:
  7.2 129.4 %copy-start = (bf16[1600,256]{1,0:T(8,128)(2,1)S(1)}, bf16[1600,256]{1,0:T(8,128)(2,1)}, u32[]{:S(2)}) copy-start(bf16[1600,256]{1,0:T(8,128)(2,1)} %param.12) | copy-start | bytes 2457604
  7.2 151.6 %all-gather.6.cloned.1.call-start = ((), (), s32[]{:S(2)}) async-start(), calls=%async_computation.1 | async-start | bytes 4259840 | tf_op jit(solution)/shard_map/all_gather | solution.py:57
  40.3 17.2 %collective-permute-start = (bf16[1600,256]{1,0:T(8,128)(2,1)}, bf16[1600,256]{1,0:T(8,128)(2,1)S(1)}, u32[]{:S(2)}, u32[]{:S(2)}) collective-permute-start(bf16[1600,256]{1,0:T(8,128)(2,1)} %param.12), channel_id=1, source_target_pairs={{0,1},{1,2},{2,3},{3,4},{4,5},{5,6},{6,7},{7,0},{8,9},{9,10},{10,1... | collective-permute-start | bytes 2457608 | tf_op jit(solution)/shard_map/ppermute | solution.py:71
  57.6 16.7 %collective-permute-start.1 = (bf16[1600,256]{1,0:T(8,128)(2,1)S(1)}, bf16[1600,256]{1,0:T(8,128)(2,1)S(1)}, u32[]{:S(2)}, u32[]{:S(2)}) collective-permute-start(bf16[1600,256]{1,0:T(8,128)(2,1)S(1)} %collective-permute-done), channel_id=1, source_target_pairs={{0,1},{1,2},{2,3},{3,4},{4,5},{5,6},{6,7},{7,0},{8,9},{9,10},{10,1... | collective-permute-start | bytes 2457608 | tf_op jit(solution)/shard_map/ppermute | solution.py:71
  59.5 16.7 %collective-permute-start.4 = (bf16[1600,256]{1,0:T(8,128)(2,1)}, bf16[1600,256]{1,0:T(8,128)(2,1)S(1)}, u32[]{:S(2)}, u32[]{:S(2)}) collective-permute-start(bf16[1600,256]{1,0:T(8,128)(2,1)} %param.12), channel_id=1, source_target_pairs={{1,0},{2,1},{3,2},{4,3},{5,4},{6,5},{7,6},{0,7},{9,8},{10,9},{11,1... | collective-permute-start | bytes 2457608 | tf_op jit(solution)/shard_map/ppermute | solution.py:73
  74.3 16.8 %collective-permute-start.2 = (bf16[1600,256]{1,0:T(8,128)(2,1)S(1)}, bf16[1600,256]{1,0:T(8,128)(2,1)}, u32[]{:S(2)}, u32[]{:S(2)}) collective-permute-start(bf16[1600,256]{1,0:T(8,128)(2,1)S(1)} %collective-permute-done.1), channel_id=1, source_target_pairs={{0,1},{1,2},{2,3},{3,4},{4,5},{5,6},{6,7},{7,0},{8,9},{9,10},{10,1... | collective-permute-start | bytes 2457608 | tf_op jit(solution)/shard_map/ppermute | solution.py:71
  76.2 49.2 %collective-permute-start.5 = (bf16[1600,256]{1,0:T(8,128)(2,1)S(1)}, bf16[1600,256]{1,0:T(8,128)(2,1)}, u32[]{:S(2)}, u32[]{:S(2)}) collective-permute-start(bf16[1600,256]{1,0:T(8,128)(2,1)S(1)} %collective-permute-done.4), channel_id=1, source_target_pairs={{1,0},{2,1},{3,2},{4,3},{5,4},{6,5},{7,6},{0,7},{9,8},{10,9},{11,1... | collective-permute-start | bytes 2457608 | tf_op jit(solution)/shard_map/ppermute | solution.py:73
  91.1 39.4 %collective-permute-start.3 = (bf16[1600,256]{1,0:T(8,128)(2,1)}, bf16[1600,256]{1,0:T(8,128)(2,1)}, u32[]{:S(2)}, u32[]{:S(2)}) collective-permute-start(bf16[1600,256]{1,0:T(8,128)(2,1)} %collective-permute-done.2), channel_id=1, source_target_pairs={{0,1},{1,2},{2,3},{3,4},{4,5},{5,6},{6,7},{7,0},{8,9},{9,10},{10,1... | collective-permute-start | bytes 2457608 | tf_op jit(solution)/shard_map/ppermute | solution.py:71
  125.4 19.4 %collective-permute-start.6 = (bf16[1600,256]{1,0:T(8,128)(2,1)}, bf16[1600,256]{1,0:T(8,128)(2,1)S(1)}, u32[]{:S(2)}, u32[]{:S(2)}) collective-permute-start(bf16[1600,256]{1,0:T(8,128)(2,1)} %collective-permute-done.5), channel_id=1, source_target_pairs={{1,0},{2,1},{3,2},{4,3},{5,4},{6,5},{7,6},{0,7},{9,8},{10,9},{11,1... | collective-permute-start | bytes 2457608 | tf_op jit(solution)/shard_map/ppermute | solution.py:73
  158.8 177.0 %copy-start.3 = (s32[16]{0:T(128)S(1)}, s32[16]{0:T(128)}, u32[]{:S(2)}) copy-start(s32[16]{0:T(128)} %param.14) | copy-start | bytes 196
  158.8 274.6 %copy-start.2 = (s32[64]{0:T(128)S(1)}, s32[64]{0:T(128)}, u32[]{:S(2)}) copy-start(s32[64]{0:T(128)} %param.15) | copy-start | bytes 772
  336.3 97.5 %copy-start.1 = (f32[16]{0:T(128)}, f32[16]{0:T(128)S(1)}, u32[]{:S(2)}) copy-start(f32[16]{0:T(128)S(1)} %get-tuple-element.158) | copy-start | bytes 196
Sparse Core Ops, SparseCore 0:
  40.5 85.8 all-gather.5
